TPU v7x, 32 devices: a whole 2x2x4 slice. The times are simulated.
32 devices in a mesh: groups: 2 (over y), shot: 4 (over z), slab: 4 (over x, core).
Axes of the slice: x: 2, y: 2, z: 4, core: 2. Of those that a mesh axis runs over, the one named last changes fastest.
Arguments:
- model: float32 [64, 64, 128], P(('groups', 'slab')), parts along dimension 0, may hold values from 0.05 to 0.3
- fwd_now: float32 [8, 32, 64, 128], P(('groups', 'shot'), 'slab'), parts along dimension 0, may hold values from -6 to 6
- fwd_next: float32 [8, 32, 64, 128], P(('groups', 'shot'), 'slab'), parts along dimension 0, may hold values from -6 to 6
- adj_now: float32 [8, 32, 64, 128], P(('groups', 'shot'), 'slab'), parts along dimension 0, may hold values from -6 to 6
- adj_next: float32 [8, 32, 64, 128], P(('groups', 'shot'), 'slab'), parts along dimension 0, may hold values from -6 to 6
- wavelet: float32 [8, 8], P(('groups', 'shot')), parts along dimension 0, may hold values from -16 to 16
- misfit: float32 [8, 8, 128], P(('groups', 'shot')), parts along dimension 0, may hold values from -6 to 6
- src_index: int32 [8], P(('groups', 'shot')), parts along dimension 0, may hold values from 0 to 262143
- rec_index: int32 [8, 128], P(('groups', 'shot')), parts along dimension 0, may hold values from 0 to 262143
Outputs:
- new_model: float32 [64, 64, 128], P(('groups', 'slab')), parts along dimension 0
- stepped: float32 [8, 32, 64, 128], P(('groups', 'shot'), 'slab'), parts along dimension 0
- adjoint_start: float32 [8, 32, 64, 128], P(('groups', 'shot'), 'slab'), parts along dimension 0
There are 2 independent parts, one for each index of `groups`. A program takes and returns all parts, laid end to end along the dimension named above; each array names one. Nothing has to cross between parts.
All inputs are finite; a program needn't handle non-finite values. Where the computation divides by a largest or mean magnitude, that divisor is 1e-20 or more.
Results may differ from a plain program's by a relative error of at most 0.00002.
Values sent between devices are 32-bit elements; how exact they have to be, the bound alone decides.
No kernel may reach another device: no remote copies, remote signals or barrier semaphores. Data moves between devices by JAX's collectives and lax.ppermute only.
A program may use at most 64 MiB of HBM per device.

v0:
```python
import jax
import jax.numpy as jnp
from jax import lax
from jax.sharding import PartitionSpec as P

ITERS = 8


def extended(block, sides, width):
    for axis, dim in sides:
        count = lax.axis_size(axis)
        forward = [(i, i + 1) for i in range(count - 1)]
        backward = [(target, source) for source, target in forward]
        low = lax.ppermute(
            lax.slice_in_dim(block, block.shape[dim] - width, None, axis=dim), axis, forward
        )
        high = lax.ppermute(lax.slice_in_dim(block, 0, width, axis=dim), axis, backward)
        block = jnp.concatenate([low, block, high], axis=dim)
    return block


def local_laplace(padded):
    full = jnp.pad(padded, ((0, 0), (0, 0), (1, 1), (1, 1)))
    center = full[:, 1:-1, 1:-1, 1:-1]
    beside = full[:, 2:, 1:-1, 1:-1] + full[:, :-2, 1:-1, 1:-1]
    beside = beside + full[:, 1:-1, 2:, 1:-1] + full[:, 1:-1, :-2, 1:-1]
    beside = beside + full[:, 1:-1, 1:-1, 2:] + full[:, 1:-1, 1:-1, :-2]
    return beside - 6.0 * center


def inject(field, index, values, offset):
    shots = field.shape[0]
    cells = field.shape[1] * field.shape[2] * field.shape[3]
    flat = field.reshape(shots, -1)
    local = index - offset
    valid = (local >= 0) & (local < cells)
    local = jnp.clip(local, 0, cells - 1)
    rows = jnp.arange(shots, dtype=jnp.int32).reshape((shots,) + (1,) * (index.ndim - 1))
    rows = jnp.broadcast_to(rows, index.shape)
    flat = flat.at[rows, local].add(jnp.where(valid, values, 0.0))
    return flat.reshape(field.shape)


def update(model, gradient, peak):
    return jnp.clip(model - 0.1 * gradient / (peak + 1e-06), 0.05, 0.3)


def per_device(model, fwd_now, fwd_next, adj_now, adj_next, wavelet, misfit, src_index, rec_index):
    shots = fwd_now.shape[0]
    depth, width, length = model.shape
    offset = lax.axis_index("slab") * (depth * width * length)
    wave, wave_later = (fwd_now, fwd_next)
    adjoint, adjoint_later = (adj_now, adj_next)
    image = jnp.zeros_like(fwd_now)
    for step in range(ITERS):
        stacked = jnp.concatenate([wave, adjoint], axis=0)
        padded = extended(stacked, (("slab", 1),), 1)
        laps = local_laplace(padded)
        lap_wave = laps[:shots]
        lap_adjoint = laps[shots:]
        image = image + adjoint * lap_wave
        wave_prior = 2.0 * wave - wave_later + model[None] * lap_wave
        wave_prior = inject(wave_prior, src_index, wavelet[:, step], offset)
        adjoint_prior = 2.0 * adjoint - adjoint_later + model[None] * lap_adjoint
        adjoint_prior = inject(adjoint_prior, rec_index, misfit[:, step, :], offset)
        wave_later, wave = (wave, wave_prior)
        adjoint_later, adjoint = (adjoint, adjoint_prior)
    local_image = jnp.sum(image, axis=0)
    gradient = lax.psum(local_image, "shot")
    peak = lax.pmax(jnp.max(jnp.abs(gradient)), "slab")
    new_model = update(model, gradient, peak)
    padded_wave = extended(wave, (("slab", 1),), 1)
    stepped = 2.0 * wave - wave_later + new_model[None] * local_laplace(padded_wave)
    return (new_model, stepped, adjoint)


def solution(mesh):
    in_specs = (
        P(("groups", "slab"), None, None),
        P(("groups", "shot"), "slab", None, None),
        P(("groups", "shot"), "slab", None, None),
        P(("groups", "shot"), "slab", None, None),
        P(("groups", "shot"), "slab", None, None),
        P(("groups", "shot"), None),
        P(("groups", "shot"), None, None),
        P(("groups", "shot")),
        P(("groups", "shot"), None),
    )
    out_specs = (
        P(("groups", "slab"), None, None),
        P(("groups", "shot"), "slab", None, None),
        P(("groups", "shot"), "slab", None, None),
    )
    return jax.shard_map(
        per_device, mesh=mesh, in_specs=in_specs, out_specs=out_specs, check_vma=False
    )
```

profile of v0, /device:TPU:0, one launch (start us, length us, event | category | flops | bytes accessed | tf_op | source)
XLA Modules:
  0.0 169.2 jit_solution(971231168128775817)
XLA Ops:
  7.2 1.0 constant_dynamic-update-slice_fusion.1
  8.2 1.0 constant_dynamic-update-slice_fusion
  9.2 2.4 %collective-permute-start.1 = (f32[2,1,64,128]{3,2,1,0:T(8,128)S(1)}, f32[2,1,64,128]{3,2,1,0:T(8,128)S(1)}, u32[]{:S(2)}, u32[]{:S(2)}) collective-permute-start(f32[2,1,64,128]{3,2,1,0:T(8,128)S(1)} %get-tuple-element.133), channel_id=1, source_target_pairs={{0,1},{1,2},{2,3},{4,5},{5,6},{6,7},{8,9},{9,10},{10,11},{12,13},{... | collective-permute-start | bytes 196616 | tf_op jit(solution)/shard_map/ppermute | solution.py:14
  11.6 1.3 collective-permute-start
  13.5 0.7 fusion.64
  14.2 0.7 fusion.65
  14.9 0.9 fusion.66
  15.9 1.6 fusion.75
  18.2 0.7 and_reduce_fusion
  23.4 1.4 scatter_fusion
  24.8 5.1 %collective-permute-start.3 = (f32[2,1,64,128]{3,2,1,0:T(8,128)S(1)}, f32[2,1,64,128]{3,2,1,0:T(8,128)S(1)}, u32[]{:S(2)}, u32[]{:S(2)}) collective-permute-start(f32[2,1,64,128]{3,2,1,0:T(8,128)S(1)} %get-tuple-element.131), channel_id=1, source_target_pairs={{0,1},{1,2},{2,3},{4,5},{5,6},{6,7},{8,9},{9,10},{10,11},{12,13},{... | collective-permute-start | bytes 196616 | tf_op jit(solution)/shard_map/ppermute | solution.py:14
  29.9 1.3 collective-permute-start.2
  31.9 2.4 %collective-permute-done.2 = f32[2,1,64,128]{3,2,1,0:T(8,128)S(1)} collective-permute-done((f32[2,1,64,128]{3,2,1,0:T(8,128)S(1)}, f32[2,1,64,128]{3,2,1,0:T(8,128)S(1)}, u32[]{:S(2)}, u32[]{:S(2)}) %collective-permute-start.2) | collective-permute-done | bytes 65568 | tf_op jit(solution)/shard_map/ppermute | solution.py:17
  38.0 1.4 scatter_fusion.1
  39.4 4.8 %collective-permute-start.5 = (f32[2,1,64,128]{3,2,1,0:T(8,128)S(1)}, f32[2,1,64,128]{3,2,1,0:T(8,128)S(1)}, u32[]{:S(2)}, u32[]{:S(2)}) collective-permute-start(f32[2,1,64,128]{3,2,1,0:T(8,128)S(1)} %get-tuple-element.129), channel_id=1, source_target_pairs={{0,1},{1,2},{2,3},{4,5},{5,6},{6,7},{8,9},{9,10},{10,11},{12,13},{... | collective-permute-start | bytes 196616 | tf_op jit(solution)/shard_map/ppermute | solution.py:14
  44.3 1.3 collective-permute-start.4
  46.1 1.3 collective-permute-done.4
  51.1 1.4 scatter_fusion.2
  52.6 4.3 %collective-permute-start.7 = (f32[2,1,64,128]{3,2,1,0:T(8,128)S(1)}, f32[2,1,64,128]{3,2,1,0:T(8,128)S(1)}, u32[]{:S(2)}, u32[]{:S(2)}) collective-permute-start(f32[2,1,64,128]{3,2,1,0:T(8,128)S(1)} %get-tuple-element.127), channel_id=1, source_target_pairs={{0,1},{1,2},{2,3},{4,5},{5,6},{6,7},{8,9},{9,10},{10,11},{12,13},{... | collective-permute-start | bytes 196616 | tf_op jit(solution)/shard_map/ppermute | solution.py:14
  56.9 1.3 collective-permute-start.6
  58.8 1.3 collective-permute-done.6
  63.8 1.4 scatter_fusion.3
  65.2 4.3 %collective-permute-start.9 = (f32[2,1,64,128]{3,2,1,0:T(8,128)S(1)}, f32[2,1,64,128]{3,2,1,0:T(8,128)S(1)}, u32[]{:S(2)}, u32[]{:S(2)}) collective-permute-start(f32[2,1,64,128]{3,2,1,0:T(8,128)S(1)} %get-tuple-element.125), channel_id=1, source_target_pairs={{0,1},{1,2},{2,3},{4,5},{5,6},{6,7},{8,9},{9,10},{10,11},{12,13},{... | collective-permute-start | bytes 196616 | tf_op jit(solution)/shard_map/ppermute | solution.py:14
  69.5 1.3 collective-permute-start.8
  71.5 1.2 collective-permute-done.8
  73.8 0.7 fusion.80
  76.5 1.4 scatter_fusion.4
  77.9 4.3 %collective-permute-start.11 = (f32[2,1,64,128]{3,2,1,0:T(8,128)S(1)}, f32[2,1,64,128]{3,2,1,0:T(8,128)S(1)}, u32[]{:S(2)}, u32[]{:S(2)}) collective-permute-start(f32[2,1,64,128]{3,2,1,0:T(8,128)S(1)} %get-tuple-element.123), channel_id=1, source_target_pairs={{0,1},{1,2},{2,3},{4,5},{5,6},{6,7},{8,9},{9,10},{10,11},{12,13},{... | collective-permute-start | bytes 196616 | tf_op jit(solution)/shard_map/ppermute | solution.py:14
  82.2 1.5 collective-permute-start.10
  84.4 1.0 collective-permute-done.10
  89.1 1.4 scatter_fusion.5
  90.5 4.3 %collective-permute-start.13 = (f32[2,1,64,128]{3,2,1,0:T(8,128)S(1)}, f32[2,1,64,128]{3,2,1,0:T(8,128)S(1)}, u32[]{:S(2)}, u32[]{:S(2)}) collective-permute-start(f32[2,1,64,128]{3,2,1,0:T(8,128)S(1)} %get-tuple-element.121), channel_id=1, source_target_pairs={{0,1},{1,2},{2,3},{4,5},{5,6},{6,7},{8,9},{9,10},{10,11},{12,13},{... | collective-permute-start | bytes 196616 | tf_op jit(solution)/shard_map/ppermute | solution.py:14
  94.9 1.3 collective-permute-start.12
  96.9 1.2 collective-permute-done.12
  101.8 1.4 scatter_fusion.6
  103.2 4.3 %collective-permute-start.15 = (f32[2,1,64,128]{3,2,1,0:T(8,128)S(1)}, f32[2,1,64,128]{3,2,1,0:T(8,128)S(1)}, u32[]{:S(2)}, u32[]{:S(2)}) collective-permute-start(f32[2,1,64,128]{3,2,1,0:T(8,128)S(1)} %get-tuple-element.119), channel_id=1, source_target_pairs={{0,1},{1,2},{2,3},{4,5},{5,6},{6,7},{8,9},{9,10},{10,11},{12,13},{... | collective-permute-start | bytes 196616 | tf_op jit(solution)/shard_map/ppermute | solution.py:14
  107.5 1.3 collective-permute-start.14
  109.5 1.2 collective-permute-done.14
  113.0 1.2 fusion.29
  114.2 1.0 fusion.48
  115.3 0.7 fusion.83
  118.0 4.4 %collective-permute-start.17 = (f32[1,1,64,128]{3,2,1,0:T(8,128)S(1)}, f32[1,1,64,128]{3,2,1,0:T(8,128)S(1)}, u32[]{:S(2)}, u32[]{:S(2)}) collective-permute-start(f32[1,1,64,128]{3,2,1,0:T(8,128)S(1)} %get-tuple-element.135), channel_id=1, source_target_pairs={{0,1},{1,2},{2,3},{4,5},{5,6},{6,7},{8,9},{9,10},{10,11},{12,13},{... | collective-permute-start | bytes 98312 | tf_op jit(solution)/shard_map/ppermute | solution.py:14
  122.4 1.3 collective-permute-start.16
  123.7 1.4 scatter_fusion.7
  125.1 27.3 %all-reduce.12.cloned.1.call-done = f32[8,64,128]{2,1,0:T(8,128)} async-done(((f32[8,64,128]{2,1,0:T(8,128)}), f32[8,64,128]{2,1,0:T(8,128)}) %all-reduce.12.cloned.1.call-update) | async-done | bytes 262160 | tf_op jit(solution)/shard_map/psum | solution.py:69
  152.4 1.6 abs_reduce_fusion
  154.3 6.3 %pmax.7 = f32[]{:T(128)} all-reduce(f32[]{:T(128)} %abs_reduce_fusion), channel_id=1, replica_groups=mesh['groups'=2,'shot'=4,'slab'=4] {'slab'}, use_global_device_ids=true, to_apply=%region_10.11 | all-reduce | flops 1 | bytes 8 | tf_op jit(solution)/shard_map/pmax | solution.py:70
  161.3 1.1 fusion.32
  (106 shorter events, 15.9 us)
Async XLA Ops:
  7.2 145.2 %all-reduce.12.cloned.1.call-start = ((), (), s32[]{:S(2)}) async-start(), calls=%async_computation | async-start | bytes 524288 | tf_op jit(solution)/shard_map/psum | solution.py:69
  9.2 9.7 %collective-permute-start.1 = (f32[2,1,64,128]{3,2,1,0:T(8,128)S(1)}, f32[2,1,64,128]{3,2,1,0:T(8,128)S(1)}, u32[]{:S(2)}, u32[]{:S(2)}) collective-permute-start(f32[2,1,64,128]{3,2,1,0:T(8,128)S(1)} %get-tuple-element.133), channel_id=1, source_target_pairs={{0,1},{1,2},{2,3},{4,5},{5,6},{6,7},{8,9},{9,10},{10,11},{12,13},{... | collective-permute-start | bytes 196616 | tf_op jit(solution)/shard_map/ppermute | solution.py:14
  11.6 7.3 %collective-permute-start = (f32[2,1,64,128]{3,2,1,0:T(8,128)S(1)}, f32[2,1,64,128]{3,2,1,0:T(8,128)S(1)}, u32[]{:S(2)}, u32[]{:S(2)}) collective-permute-start(f32[2,1,64,128]{3,2,1,0:T(8,128)S(1)} %get-tuple-element.134), channel_id=1, source_target_pairs={{1,0},{2,1},{3,2},{5,4},{6,5},{7,6},{9,8},{10,9},{11,10},{13,12},{... | collective-permute-start | bytes 196616 | tf_op jit(solution)/shard_map/ppermute | solution.py:17
  19.3 1.0 copy-start
  19.3 1.0 copy-start.1
  19.4 1.1 copy-start.17
  19.4 1.2 copy-start.20
  19.4 1.2 copy-start.21
  20.6 0.8 copy-start.3
  24.8 7.1 %collective-permute-start.3 = (f32[2,1,64,128]{3,2,1,0:T(8,128)S(1)}, f32[2,1,64,128]{3,2,1,0:T(8,128)S(1)}, u32[]{:S(2)}, u32[]{:S(2)}) collective-permute-start(f32[2,1,64,128]{3,2,1,0:T(8,128)S(1)} %get-tuple-element.131), channel_id=1, source_target_pairs={{0,1},{1,2},{2,3},{4,5},{5,6},{6,7},{8,9},{9,10},{10,11},{12,13},{... | collective-permute-start | bytes 196616 | tf_op jit(solution)/shard_map/ppermute | solution.py:14
  29.9 4.4 %collective-permute-start.2 = (f32[2,1,64,128]{3,2,1,0:T(8,128)S(1)}, f32[2,1,64,128]{3,2,1,0:T(8,128)S(1)}, u32[]{:S(2)}, u32[]{:S(2)}) collective-permute-start(f32[2,1,64,128]{3,2,1,0:T(8,128)S(1)} %get-tuple-element.132), channel_id=1, source_target_pairs={{1,0},{2,1},{3,2},{5,4},{6,5},{7,6},{9,8},{10,9},{11,10},{13,12},{... | collective-permute-start | bytes 196616 | tf_op jit(solution)/shard_map/ppermute | solution.py:17
  35.3 0.8 copy-start.5
  39.4 6.7 %collective-permute-start.5 = (f32[2,1,64,128]{3,2,1,0:T(8,128)S(1)}, f32[2,1,64,128]{3,2,1,0:T(8,128)S(1)}, u32[]{:S(2)}, u32[]{:S(2)}) collective-permute-start(f32[2,1,64,128]{3,2,1,0:T(8,128)S(1)} %get-tuple-element.129), channel_id=1, source_target_pairs={{0,1},{1,2},{2,3},{4,5},{5,6},{6,7},{8,9},{9,10},{10,11},{12,13},{... | collective-permute-start | bytes 196616 | tf_op jit(solution)/shard_map/ppermute | solution.py:14
  44.3 3.1 %collective-permute-start.4 = (f32[2,1,64,128]{3,2,1,0:T(8,128)S(1)}, f32[2,1,64,128]{3,2,1,0:T(8,128)S(1)}, u32[]{:S(2)}, u32[]{:S(2)}) collective-permute-start(f32[2,1,64,128]{3,2,1,0:T(8,128)S(1)} %get-tuple-element.130), channel_id=1, source_target_pairs={{1,0},{2,1},{3,2},{5,4},{6,5},{7,6},{9,8},{10,9},{11,10},{13,12},{... | collective-permute-start | bytes 196616 | tf_op jit(solution)/shard_map/ppermute | solution.py:17
  48.4 0.8 copy-start.7
  52.6 6.2 %collective-permute-start.7 = (f32[2,1,64,128]{3,2,1,0:T(8,128)S(1)}, f32[2,1,64,128]{3,2,1,0:T(8,128)S(1)}, u32[]{:S(2)}, u32[]{:S(2)}) collective-permute-start(f32[2,1,64,128]{3,2,1,0:T(8,128)S(1)} %get-tuple-element.127), channel_id=1, source_target_pairs={{0,1},{1,2},{2,3},{4,5},{5,6},{6,7},{8,9},{9,10},{10,11},{12,13},{... | collective-permute-start | bytes 196616 | tf_op jit(solution)/shard_map/ppermute | solution.py:14
  56.9 3.1 %collective-permute-start.6 = (f32[2,1,64,128]{3,2,1,0:T(8,128)S(1)}, f32[2,1,64,128]{3,2,1,0:T(8,128)S(1)}, u32[]{:S(2)}, u32[]{:S(2)}) collective-permute-start(f32[2,1,64,128]{3,2,1,0:T(8,128)S(1)} %get-tuple-element.128), channel_id=1, source_target_pairs={{1,0},{2,1},{3,2},{5,4},{6,5},{7,6},{9,8},{10,9},{11,10},{13,12},{... | collective-permute-start | bytes 196616 | tf_op jit(solution)/shard_map/ppermute | solution.py:17
  61.0 0.8 copy-start.9
  65.2 6.3 %collective-permute-start.9 = (f32[2,1,64,128]{3,2,1,0:T(8,128)S(1)}, f32[2,1,64,128]{3,2,1,0:T(8,128)S(1)}, u32[]{:S(2)}, u32[]{:S(2)}) collective-permute-start(f32[2,1,64,128]{3,2,1,0:T(8,128)S(1)} %get-tuple-element.125), channel_id=1, source_target_pairs={{0,1},{1,2},{2,3},{4,5},{5,6},{6,7},{8,9},{9,10},{10,11},{12,13},{... | collective-permute-start | bytes 196616 | tf_op jit(solution)/shard_map/ppermute | solution.py:14
  69.5 3.1 %collective-permute-start.8 = (f32[2,1,64,128]{3,2,1,0:T(8,128)S(1)}, f32[2,1,64,128]{3,2,1,0:T(8,128)S(1)}, u32[]{:S(2)}, u32[]{:S(2)}) collective-permute-start(f32[2,1,64,128]{3,2,1,0:T(8,128)S(1)} %get-tuple-element.126), channel_id=1, source_target_pairs={{1,0},{2,1},{3,2},{5,4},{6,5},{7,6},{9,8},{10,9},{11,10},{13,12},{... | collective-permute-start | bytes 196616 | tf_op jit(solution)/shard_map/ppermute | solution.py:17
  73.6 0.8 copy-start.11
  77.9 6.5 %collective-permute-start.11 = (f32[2,1,64,128]{3,2,1,0:T(8,128)S(1)}, f32[2,1,64,128]{3,2,1,0:T(8,128)S(1)}, u32[]{:S(2)}, u32[]{:S(2)}) collective-permute-start(f32[2,1,64,128]{3,2,1,0:T(8,128)S(1)} %get-tuple-element.123), channel_id=1, source_target_pairs={{0,1},{1,2},{2,3},{4,5},{5,6},{6,7},{8,9},{9,10},{10,11},{12,13},{... | collective-permute-start | bytes 196616 | tf_op jit(solution)/shard_map/ppermute | solution.py:14
  82.2 3.1 %collective-permute-start.10 = (f32[2,1,64,128]{3,2,1,0:T(8,128)S(1)}, f32[2,1,64,128]{3,2,1,0:T(8,128)S(1)}, u32[]{:S(2)}, u32[]{:S(2)}) collective-permute-start(f32[2,1,64,128]{3,2,1,0:T(8,128)S(1)} %get-tuple-element.124), channel_id=1, source_target_pairs={{1,0},{2,1},{3,2},{5,4},{6,5},{7,6},{9,8},{10,9},{11,10},{13,12},{... | collective-permute-start | bytes 196616 | tf_op jit(solution)/shard_map/ppermute | solution.py:17
  86.4 0.8 copy-start.13
  90.5 6.3 %collective-permute-start.13 = (f32[2,1,64,128]{3,2,1,0:T(8,128)S(1)}, f32[2,1,64,128]{3,2,1,0:T(8,128)S(1)}, u32[]{:S(2)}, u32[]{:S(2)}) collective-permute-start(f32[2,1,64,128]{3,2,1,0:T(8,128)S(1)} %get-tuple-element.121), channel_id=1, source_target_pairs={{0,1},{1,2},{2,3},{4,5},{5,6},{6,7},{8,9},{9,10},{10,11},{12,13},{... | collective-permute-start | bytes 196616 | tf_op jit(solution)/shard_map/ppermute | solution.py:14
  94.9 3.1 %collective-permute-start.12 = (f32[2,1,64,128]{3,2,1,0:T(8,128)S(1)}, f32[2,1,64,128]{3,2,1,0:T(8,128)S(1)}, u32[]{:S(2)}, u32[]{:S(2)}) collective-permute-start(f32[2,1,64,128]{3,2,1,0:T(8,128)S(1)} %get-tuple-element.122), channel_id=1, source_target_pairs={{1,0},{2,1},{3,2},{5,4},{6,5},{7,6},{9,8},{10,9},{11,10},{13,12},{... | collective-permute-start | bytes 196616 | tf_op jit(solution)/shard_map/ppermute | solution.py:17
  99.0 0.8 copy-start.15
  103.2 6.3 %collective-permute-start.15 = (f32[2,1,64,128]{3,2,1,0:T(8,128)S(1)}, f32[2,1,64,128]{3,2,1,0:T(8,128)S(1)}, u32[]{:S(2)}, u32[]{:S(2)}) collective-permute-start(f32[2,1,64,128]{3,2,1,0:T(8,128)S(1)} %get-tuple-element.119), channel_id=1, source_target_pairs={{0,1},{1,2},{2,3},{4,5},{5,6},{6,7},{8,9},{9,10},{10,11},{12,13},{... | collective-permute-start | bytes 196616 | tf_op jit(solution)/shard_map/ppermute | solution.py:14
  107.5 3.1 %collective-permute-start.14 = (f32[2,1,64,128]{3,2,1,0:T(8,128)S(1)}, f32[2,1,64,128]{3,2,1,0:T(8,128)S(1)}, u32[]{:S(2)}, u32[]{:S(2)}) collective-permute-start(f32[2,1,64,128]{3,2,1,0:T(8,128)S(1)} %get-tuple-element.120), channel_id=1, source_target_pairs={{1,0},{2,1},{3,2},{5,4},{6,5},{7,6},{9,8},{10,9},{11,10},{13,12},{... | collective-permute-start | bytes 196616 | tf_op jit(solution)/shard_map/ppermute | solution.py:17
  110.7 1.0 copy-start.16
  111.2 1.1 copy-start.4
  111.2 1.2 copy-start.6
  111.2 1.4 copy-start.8
  111.2 1.5 copy-start.10
  111.2 1.7 copy-start.12
  111.2 1.8 %copy-start.14 = (f32[2,8,64,128]{3,2,1,0:T(8,128)S(1)}, f32[2,8,64,128]{3,2,1,0:T(8,128)}, u32[]{:S(2)}) copy-start(f32[2,8,64,128]{3,2,1,0:T(8,128)} %copy-done.13) | copy-start | bytes 1572868
  113.0 1.2 copy-start.2
  118.0 36.0 %collective-permute-start.17 = (f32[1,1,64,128]{3,2,1,0:T(8,128)S(1)}, f32[1,1,64,128]{3,2,1,0:T(8,128)S(1)}, u32[]{:S(2)}, u32[]{:S(2)}) collective-permute-start(f32[1,1,64,128]{3,2,1,0:T(8,128)S(1)} %get-tuple-element.135), channel_id=1, source_target_pairs={{0,1},{1,2},{2,3},{4,5},{5,6},{6,7},{8,9},{9,10},{10,11},{12,13},{... | collective-permute-start | bytes 98312 | tf_op jit(solution)/shard_map/ppermute | solution.py:14
  122.4 31.6 %collective-permute-start.16 = (f32[1,1,64,128]{3,2,1,0:T(8,128)S(1)}, f32[1,1,64,128]{3,2,1,0:T(8,128)S(1)}, u32[]{:S(2)}, u32[]{:S(2)}) collective-permute-start(f32[1,1,64,128]{3,2,1,0:T(8,128)S(1)} %get-tuple-element.136), channel_id=1, source_target_pairs={{1,0},{2,1},{3,2},{5,4},{6,5},{7,6},{9,8},{10,9},{11,10},{13,12},{... | collective-permute-start | bytes 98312 | tf_op jit(solution)/shard_map/ppermute | solution.py:17
  125.1 37.2 %copy-start.18 = (f32[65536]{0:T(1024)}, f32[65536]{0:T(1024)S(1)}, u32[]{:S(2)}) copy-start(f32[65536]{0:T(1024)S(1)} %scatter_fusion.7) | copy-start | bytes 786436
  152.4 8.9 %copy-start.19 = (f32[8,64,128]{2,1,0:T(8,128)S(1)}, f32[8,64,128]{2,1,0:T(8,128)}, u32[]{:S(2)}) copy-start(f32[8,64,128]{2,1,0:T(8,128)} %all-reduce.12.cloned.1.call-done) | copy-start | bytes 786436
Sparse Core Ops, SparseCore 0:
  114.4 37.9 all-reduce.11
where the time goes:
time: 170 us; the launch traced here: 169 us
  starting transfers between devices  50.2 us (30%)
  waiting for transfers between devices  36.8 us (22%)
  between operations  36 us (21%)
  other arithmetic  33.2 us (20%)
  local copies, waits for them, and re-layouts  6.66 us (4%)
  blocking collectives  6.3 us (4%)
    ppermute x9, starting transfers between devices, extended(): lax.ppermute(lax.slice_in_dim(block, block.shape[dim] - width, None, axis...  38.4 us
    psum x1, waiting for transfers between devices, per_device(): gradient = lax.psum(local_image, 'shot')  27.3 us
    ppermute x9, starting transfers between devices, extended(): lax.ppermute(lax.slice_in_dim(block, 0, width, axis=dim), axis, backward)  11.8 us
    scatter-add x8, other arithmetic, inject(): flat = flat.at[rows, local].add(jnp.where(valid, values, 0.0))  11.2 us
    ppermute x9, waiting for transfers between devices, extended(): lax.ppermute(lax.slice_in_dim(block, 0, width, axis=dim), axis, backward)  9.49 us
    pmax x1, blocking collectives, per_device(): peak = lax.pmax(jnp.max(jnp.abs(gradient)), 'slab')  6.3 us
    add x8, other arithmetic, inject(): flat = flat.at[rows, local].add(jnp.where(valid, values, 0.0))  5.13 us
    sub x8, other arithmetic, local_laplace(): return beside - 6.0 * center  4.02 us
  transfers between devices with their start and end apart: 19, of which 8 were waited for; matrix products, arithmetic and copies ran while one was open for 6% of the time, Pallas kernels for 0%

commit v1 on v0

--- a/solution.py
+++ b/solution.py
@@ -4,6 +4,12 @@
 from jax.sharding import PartitionSpec as P
 
 ITERS = 8
+
+
+def summed_here(x, mesh_axis):
+    parts = lax.all_gather(x, mesh_axis, axis=0, tiled=False)
+    result = parts.sum(axis=0)
+    return result
 
 
 def extended(block, sides, width):
@@ -66,7 +72,7 @@
         wave_later, wave = (wave, wave_prior)
         adjoint_later, adjoint = (adjoint, adjoint_prior)
     local_image = jnp.sum(image, axis=0)
-    gradient = lax.psum(local_image, "shot")
+    gradient = summed_here(local_image, "shot")
     peak = lax.pmax(jnp.max(jnp.abs(gradient)), "slab")
     new_model = update(model, gradient, peak)
     padded_wave = extended(wave, (("slab", 1),), 1)

time: 170 us -> 164 us (0.965)
  waiting for transfers between devices: 36.8 us -> 29.5 us
    psum x1 -> x0, waiting for transfers between devices: 27.3 us -> none  [per_device(): gradient = lax.psum(local_image, 'shot')]
    all_gather x0 -> x1, waiting for transfers between devices: none -> 19.2 us  [summed_here(): parts = lax.all_gather(x, mesh_axis, axis=0, tiled=False)]
where the time goes in v1:
time: 164 us; the launch traced here: 163 us
  starting transfers between devices  50.2 us (31%)
  between operations  36.2 us (22%)
  other arithmetic  33.6 us (20%)
  waiting for transfers between devices  29.5 us (18%)
  blocking collectives  6.72 us (4%)
  local copies, waits for them, and re-layouts  6.63 us (4%)
    ppermute x9, starting transfers between devices, extended(): lax.ppermute(lax.slice_in_dim(block, block.shape[dim] - width, None, axis...  38.4 us
    all_gather x1, waiting for transfers between devices, summed_here(): parts = lax.all_gather(x, mesh_axis, axis=0, tiled=False)  19.2 us
    ppermute x9, starting transfers between devices, extended(): lax.ppermute(lax.slice_in_dim(block, 0, width, axis=dim), axis, backward)  11.8 us
    scatter-add x8, other arithmetic, inject(): flat = flat.at[rows, local].add(jnp.where(valid, values, 0.0))  11.2 us
    ppermute x9, waiting for transfers between devices, extended(): lax.ppermute(lax.slice_in_dim(block, 0, width, axis=dim), axis, backward)  10.2 us
    pmax x1, blocking collectives, per_device(): peak = lax.pmax(jnp.max(jnp.abs(gradient)), 'slab')  6.72 us
    add x8, other arithmetic, inject(): flat = flat.at[rows, local].add(jnp.where(valid, values, 0.0))  5.27 us
    sub x8, other arithmetic, local_laplace(): return beside - 6.0 * center  4.02 us
  transfers between devices with their start and end apart: 19, of which 8 were waited for; matrix products, arithmetic and copies ran while one was open for 6% of the time, Pallas kernels for 0%

profile of v1, /device:TPU:0, one launch (start us, length us, event | category | flops | bytes accessed | tf_op | source)
XLA Modules:
  0.0 162.8 jit_solution(2310037785842486905)
XLA Ops:
  7.2 1.0 constant_dynamic-update-slice_fusion.1
  8.2 1.0 constant_dynamic-update-slice_fusion
  9.2 2.4 %collective-permute-start.1 = (f32[2,1,64,128]{3,2,1,0:T(8,128)S(1)}, f32[2,1,64,128]{3,2,1,0:T(8,128)S(1)}, u32[]{:S(2)}, u32[]{:S(2)}) collective-permute-start(f32[2,1,64,128]{3,2,1,0:T(8,128)S(1)} %get-tuple-element.133), channel_id=1, source_target_pairs={{0,1},{1,2},{2,3},{4,5},{5,6},{6,7},{8,9},{9,10},{10,11},{12,13},{... | collective-permute-start | bytes 196616 | tf_op jit(solution)/shard_map/ppermute | solution.py:20
  11.6 1.3 collective-permute-start
  14.2 0.7 fusion.65
  14.9 0.9 fusion.66
  15.9 1.6 %fusion.75 = (f32[1,1]{1,0:T(1,128)}, f32[1,1]{1,0:T(1,128)}, f32[1,1]{1,0:T(1,128)}, f32[1,1]{1,0:T(1,128)}, f32[1,1]{1,0:T(1,128)}, /*index=5*/f32[1,1]{1,0:T(1,128)}, f32[1,1]{1,0:T(1,128)}, f32[1,1]{1,0:T(1,128)}) fusion(f32[1,8]{1,0:T(1,128)} %param.30), kind=kLoop, calls=%fused_computation.261 | loop fusion | bytes 64 | tf_op jit(solution)/shard_map/slice | solution.py:69
  18.2 0.7 and_reduce_fusion
  20.8 0.7 fusion.76
  23.5 1.4 scatter_fusion
  24.9 5.1 %collective-permute-start.3 = (f32[2,1,64,128]{3,2,1,0:T(8,128)S(1)}, f32[2,1,64,128]{3,2,1,0:T(8,128)S(1)}, u32[]{:S(2)}, u32[]{:S(2)}) collective-permute-start(f32[2,1,64,128]{3,2,1,0:T(8,128)S(1)} %get-tuple-element.131), channel_id=1, source_target_pairs={{0,1},{1,2},{2,3},{4,5},{5,6},{6,7},{8,9},{9,10},{10,11},{12,13},{... | collective-permute-start | bytes 196616 | tf_op jit(solution)/shard_map/ppermute | solution.py:20
  30.0 1.3 collective-permute-start.2
  31.9 2.5 %collective-permute-done.2 = f32[2,1,64,128]{3,2,1,0:T(8,128)S(1)} collective-permute-done((f32[2,1,64,128]{3,2,1,0:T(8,128)S(1)}, f32[2,1,64,128]{3,2,1,0:T(8,128)S(1)}, u32[]{:S(2)}, u32[]{:S(2)}) %collective-permute-start.2) | collective-permute-done | bytes 65568 | tf_op jit(solution)/shard_map/ppermute | solution.py:23
  38.2 1.4 scatter_fusion.1
  39.7 4.8 %collective-permute-start.5 = (f32[2,1,64,128]{3,2,1,0:T(8,128)S(1)}, f32[2,1,64,128]{3,2,1,0:T(8,128)S(1)}, u32[]{:S(2)}, u32[]{:S(2)}) collective-permute-start(f32[2,1,64,128]{3,2,1,0:T(8,128)S(1)} %get-tuple-element.129), channel_id=1, source_target_pairs={{0,1},{1,2},{2,3},{4,5},{5,6},{6,7},{8,9},{9,10},{10,11},{12,13},{... | collective-permute-start | bytes 196616 | tf_op jit(solution)/shard_map/ppermute | solution.py:20
  44.5 1.3 collective-permute-start.4
  46.4 1.3 collective-permute-done.4
  51.3 1.4 scatter_fusion.2
  52.8 4.3 %collective-permute-start.7 = (f32[2,1,64,128]{3,2,1,0:T(8,128)S(1)}, f32[2,1,64,128]{3,2,1,0:T(8,128)S(1)}, u32[]{:S(2)}, u32[]{:S(2)}) collective-permute-start(f32[2,1,64,128]{3,2,1,0:T(8,128)S(1)} %get-tuple-element.127), channel_id=1, source_target_pairs={{0,1},{1,2},{2,3},{4,5},{5,6},{6,7},{8,9},{9,10},{10,11},{12,13},{... | collective-permute-start | bytes 196616 | tf_op jit(solution)/shard_map/ppermute | solution.py:20
  57.1 1.3 collective-permute-start.6
  59.0 1.3 collective-permute-done.6
  64.0 1.4 scatter_fusion.3
  65.4 4.3 %collective-permute-start.9 = (f32[2,1,64,128]{3,2,1,0:T(8,128)S(1)}, f32[2,1,64,128]{3,2,1,0:T(8,128)S(1)}, u32[]{:S(2)}, u32[]{:S(2)}) collective-permute-start(f32[2,1,64,128]{3,2,1,0:T(8,128)S(1)} %get-tuple-element.125), channel_id=1, source_target_pairs={{0,1},{1,2},{2,3},{4,5},{5,6},{6,7},{8,9},{9,10},{10,11},{12,13},{... | collective-permute-start | bytes 196616 | tf_op jit(solution)/shard_map/ppermute | solution.py:20
  69.7 1.3 collective-permute-start.8
  71.7 1.2 collective-permute-done.8
  74.0 0.7 fusion.80
  76.7 1.4 scatter_fusion.4
  78.1 4.3 %collective-permute-start.11 = (f32[2,1,64,128]{3,2,1,0:T(8,128)S(1)}, f32[2,1,64,128]{3,2,1,0:T(8,128)S(1)}, u32[]{:S(2)}, u32[]{:S(2)}) collective-permute-start(f32[2,1,64,128]{3,2,1,0:T(8,128)S(1)} %get-tuple-element.123), channel_id=1, source_target_pairs={{0,1},{1,2},{2,3},{4,5},{5,6},{6,7},{8,9},{9,10},{10,11},{12,13},{... | collective-permute-start | bytes 196616 | tf_op jit(solution)/shard_map/ppermute | solution.py:20
  82.5 1.5 collective-permute-start.10
  84.6 1.0 collective-permute-done.10
  89.5 1.4 scatter_fusion.5
  90.9 4.3 %collective-permute-start.13 = (f32[2,1,64,128]{3,2,1,0:T(8,128)S(1)}, f32[2,1,64,128]{3,2,1,0:T(8,128)S(1)}, u32[]{:S(2)}, u32[]{:S(2)}) collective-permute-start(f32[2,1,64,128]{3,2,1,0:T(8,128)S(1)} %get-tuple-element.121), channel_id=1, source_target_pairs={{0,1},{1,2},{2,3},{4,5},{5,6},{6,7},{8,9},{9,10},{10,11},{12,13},{... | collective-permute-start | bytes 196616 | tf_op jit(solution)/shard_map/ppermute | solution.py:20
  95.3 1.3 collective-permute-start.12
  97.2 1.2 collective-permute-done.12
  102.3 1.4 scatter_fusion.6
  103.7 4.3 %collective-permute-start.15 = (f32[2,1,64,128]{3,2,1,0:T(8,128)S(1)}, f32[2,1,64,128]{3,2,1,0:T(8,128)S(1)}, u32[]{:S(2)}, u32[]{:S(2)}) collective-permute-start(f32[2,1,64,128]{3,2,1,0:T(8,128)S(1)} %get-tuple-element.119), channel_id=1, source_target_pairs={{0,1},{1,2},{2,3},{4,5},{5,6},{6,7},{8,9},{9,10},{10,11},{12,13},{... | collective-permute-start | bytes 196616 | tf_op jit(solution)/shard_map/ppermute | solution.py:20
  108.1 1.3 collective-permute-start.14
  109.4 1.8 %collective-permute-done.14 = f32[2,1,64,128]{3,2,1,0:T(8,128)S(1)} collective-permute-done((f32[2,1,64,128]{3,2,1,0:T(8,128)S(1)}, f32[2,1,64,128]{3,2,1,0:T(8,128)S(1)}, u32[]{:S(2)}, u32[]{:S(2)}) %collective-permute-start.14) | collective-permute-done | bytes 65568 | tf_op jit(solution)/shard_map/ppermute | solution.py:23
  113.5 1.2 fusion.29
  115.3 1.0 fusion.48
  116.3 0.7 fusion.83
  119.0 4.4 %collective-permute-start.17 = (f32[1,1,64,128]{3,2,1,0:T(8,128)S(1)}, f32[1,1,64,128]{3,2,1,0:T(8,128)S(1)}, u32[]{:S(2)}, u32[]{:S(2)}) collective-permute-start(f32[1,1,64,128]{3,2,1,0:T(8,128)S(1)} %get-tuple-element.135), channel_id=1, source_target_pairs={{0,1},{1,2},{2,3},{4,5},{5,6},{6,7},{8,9},{9,10},{10,11},{12,13},{... | collective-permute-start | bytes 98312 | tf_op jit(solution)/shard_map/ppermute | solution.py:20
  123.4 1.3 collective-permute-start.16
  124.7 1.4 scatter_fusion.7
  126.1 19.2 %all-gather.2.cloned.1.call-done = f32[4,8,64,128]{3,2,1,0:T(8,128)} async-done(((f32[1,8,64,128]{3,2,1,0:T(8,128)}), f32[4,8,64,128]{3,2,1,0:T(8,128)}) %all-gather.2.cloned.1.call-update) | async-done | bytes 1048592 | tf_op jit(solution)/shard_map/all_gather | solution.py:10
  145.3 1.3 reduce_sum.8
  147.5 6.7 %pmax.7 = f32[]{:T(128)} all-reduce(f32[]{:T(128)} %abs_reduce_fusion), channel_id=1, replica_groups=mesh['groups'=2,'shot'=4,'slab'=4] {'slab'}, use_global_device_ids=true, to_apply=%region_10.11 | all-reduce | flops 1 | bytes 8 | tf_op jit(solution)/shard_map/pmax | solution.py:76
  154.9 1.1 fusion.32
  (105 shorter events, 16.6 us)
Async XLA Ops:
  7.2 138.1 %all-gather.2.cloned.1.call-start = ((), (), s32[]{:S(2)}) async-start(), calls=%async_computation | async-start | bytes 1310720 | tf_op jit(solution)/shard_map/all_gather | solution.py:10
  9.2 9.7 %collective-permute-start.1 = (f32[2,1,64,128]{3,2,1,0:T(8,128)S(1)}, f32[2,1,64,128]{3,2,1,0:T(8,128)S(1)}, u32[]{:S(2)}, u32[]{:S(2)}) collective-permute-start(f32[2,1,64,128]{3,2,1,0:T(8,128)S(1)} %get-tuple-element.133), channel_id=1, source_target_pairs={{0,1},{1,2},{2,3},{4,5},{5,6},{6,7},{8,9},{9,10},{10,11},{12,13},{... | collective-permute-start | bytes 196616 | tf_op jit(solution)/shard_map/ppermute | solution.py:20
  11.6 7.3 %collective-permute-start = (f32[2,1,64,128]{3,2,1,0:T(8,128)S(1)}, f32[2,1,64,128]{3,2,1,0:T(8,128)S(1)}, u32[]{:S(2)}, u32[]{:S(2)}) collective-permute-start(f32[2,1,64,128]{3,2,1,0:T(8,128)S(1)} %get-tuple-element.134), channel_id=1, source_target_pairs={{1,0},{2,1},{3,2},{5,4},{6,5},{7,6},{9,8},{10,9},{11,10},{13,12},{... | collective-permute-start | bytes 196616 | tf_op jit(solution)/shard_map/ppermute | solution.py:23
  19.3 1.0 copy-start
  19.3 1.0 copy-start.1
  19.4 1.1 copy-start.17
  19.4 1.2 copy-start.19
  19.4 1.2 copy-start.20
  20.6 0.8 copy-start.3
  24.9 7.0 %collective-permute-start.3 = (f32[2,1,64,128]{3,2,1,0:T(8,128)S(1)}, f32[2,1,64,128]{3,2,1,0:T(8,128)S(1)}, u32[]{:S(2)}, u32[]{:S(2)}) collective-permute-start(f32[2,1,64,128]{3,2,1,0:T(8,128)S(1)} %get-tuple-element.131), channel_id=1, source_target_pairs={{0,1},{1,2},{2,3},{4,5},{5,6},{6,7},{8,9},{9,10},{10,11},{12,13},{... | collective-permute-start | bytes 196616 | tf_op jit(solution)/shard_map/ppermute | solution.py:20
  30.0 4.4 %collective-permute-start.2 = (f32[2,1,64,128]{3,2,1,0:T(8,128)S(1)}, f32[2,1,64,128]{3,2,1,0:T(8,128)S(1)}, u32[]{:S(2)}, u32[]{:S(2)}) collective-permute-start(f32[2,1,64,128]{3,2,1,0:T(8,128)S(1)} %get-tuple-element.132), channel_id=1, source_target_pairs={{1,0},{2,1},{3,2},{5,4},{6,5},{7,6},{9,8},{10,9},{11,10},{13,12},{... | collective-permute-start | bytes 196616 | tf_op jit(solution)/shard_map/ppermute | solution.py:23
  35.3 0.8 copy-start.5
  39.7 6.7 %collective-permute-start.5 = (f32[2,1,64,128]{3,2,1,0:T(8,128)S(1)}, f32[2,1,64,128]{3,2,1,0:T(8,128)S(1)}, u32[]{:S(2)}, u32[]{:S(2)}) collective-permute-start(f32[2,1,64,128]{3,2,1,0:T(8,128)S(1)} %get-tuple-element.129), channel_id=1, source_target_pairs={{0,1},{1,2},{2,3},{4,5},{5,6},{6,7},{8,9},{9,10},{10,11},{12,13},{... | collective-permute-start | bytes 196616 | tf_op jit(solution)/shard_map/ppermute | solution.py:20
  44.5 3.1 %collective-permute-start.4 = (f32[2,1,64,128]{3,2,1,0:T(8,128)S(1)}, f32[2,1,64,128]{3,2,1,0:T(8,128)S(1)}, u32[]{:S(2)}, u32[]{:S(2)}) collective-permute-start(f32[2,1,64,128]{3,2,1,0:T(8,128)S(1)} %get-tuple-element.130), channel_id=1, source_target_pairs={{1,0},{2,1},{3,2},{5,4},{6,5},{7,6},{9,8},{10,9},{11,10},{13,12},{... | collective-permute-start | bytes 196616 | tf_op jit(solution)/shard_map/ppermute | solution.py:23
  48.6 0.8 copy-start.7
  52.8 6.2 %collective-permute-start.7 = (f32[2,1,64,128]{3,2,1,0:T(8,128)S(1)}, f32[2,1,64,128]{3,2,1,0:T(8,128)S(1)}, u32[]{:S(2)}, u32[]{:S(2)}) collective-permute-start(f32[2,1,64,128]{3,2,1,0:T(8,128)S(1)} %get-tuple-element.127), channel_id=1, source_target_pairs={{0,1},{1,2},{2,3},{4,5},{5,6},{6,7},{8,9},{9,10},{10,11},{12,13},{... | collective-permute-start | bytes 196616 | tf_op jit(solution)/shard_map/ppermute | solution.py:20
  57.1 3.1 %collective-permute-start.6 = (f32[2,1,64,128]{3,2,1,0:T(8,128)S(1)}, f32[2,1,64,128]{3,2,1,0:T(8,128)S(1)}, u32[]{:S(2)}, u32[]{:S(2)}) collective-permute-start(f32[2,1,64,128]{3,2,1,0:T(8,128)S(1)} %get-tuple-element.128), channel_id=1, source_target_pairs={{1,0},{2,1},{3,2},{5,4},{6,5},{7,6},{9,8},{10,9},{11,10},{13,12},{... | collective-permute-start | bytes 196616 | tf_op jit(solution)/shard_map/ppermute | solution.py:23
  61.2 0.8 copy-start.9
  65.4 6.3 %collective-permute-start.9 = (f32[2,1,64,128]{3,2,1,0:T(8,128)S(1)}, f32[2,1,64,128]{3,2,1,0:T(8,128)S(1)}, u32[]{:S(2)}, u32[]{:S(2)}) collective-permute-start(f32[2,1,64,128]{3,2,1,0:T(8,128)S(1)} %get-tuple-element.125), channel_id=1, source_target_pairs={{0,1},{1,2},{2,3},{4,5},{5,6},{6,7},{8,9},{9,10},{10,11},{12,13},{... | collective-permute-start | bytes 196616 | tf_op jit(solution)/shard_map/ppermute | solution.py:20
  69.7 3.1 %collective-permute-start.8 = (f32[2,1,64,128]{3,2,1,0:T(8,128)S(1)}, f32[2,1,64,128]{3,2,1,0:T(8,128)S(1)}, u32[]{:S(2)}, u32[]{:S(2)}) collective-permute-start(f32[2,1,64,128]{3,2,1,0:T(8,128)S(1)} %get-tuple-element.126), channel_id=1, source_target_pairs={{1,0},{2,1},{3,2},{5,4},{6,5},{7,6},{9,8},{10,9},{11,10},{13,12},{... | collective-permute-start | bytes 196616 | tf_op jit(solution)/shard_map/ppermute | solution.py:23
  73.8 0.8 copy-start.11
  78.1 6.5 %collective-permute-start.11 = (f32[2,1,64,128]{3,2,1,0:T(8,128)S(1)}, f32[2,1,64,128]{3,2,1,0:T(8,128)S(1)}, u32[]{:S(2)}, u32[]{:S(2)}) collective-permute-start(f32[2,1,64,128]{3,2,1,0:T(8,128)S(1)} %get-tuple-element.123), channel_id=1, source_target_pairs={{0,1},{1,2},{2,3},{4,5},{5,6},{6,7},{8,9},{9,10},{10,11},{12,13},{... | collective-permute-start | bytes 196616 | tf_op jit(solution)/shard_map/ppermute | solution.py:20
  82.5 3.1 %collective-permute-start.10 = (f32[2,1,64,128]{3,2,1,0:T(8,128)S(1)}, f32[2,1,64,128]{3,2,1,0:T(8,128)S(1)}, u32[]{:S(2)}, u32[]{:S(2)}) collective-permute-start(f32[2,1,64,128]{3,2,1,0:T(8,128)S(1)} %get-tuple-element.124), channel_id=1, source_target_pairs={{1,0},{2,1},{3,2},{5,4},{6,5},{7,6},{9,8},{10,9},{11,10},{13,12},{... | collective-permute-start | bytes 196616 | tf_op jit(solution)/shard_map/ppermute | solution.py:23
  86.6 0.8 copy-start.13
  90.9 6.3 %collective-permute-start.13 = (f32[2,1,64,128]{3,2,1,0:T(8,128)S(1)}, f32[2,1,64,128]{3,2,1,0:T(8,128)S(1)}, u32[]{:S(2)}, u32[]{:S(2)}) collective-permute-start(f32[2,1,64,128]{3,2,1,0:T(8,128)S(1)} %get-tuple-element.121), channel_id=1, source_target_pairs={{0,1},{1,2},{2,3},{4,5},{5,6},{6,7},{8,9},{9,10},{10,11},{12,13},{... | collective-permute-start | bytes 196616 | tf_op jit(solution)/shard_map/ppermute | solution.py:20
  95.3 3.1 %collective-permute-start.12 = (f32[2,1,64,128]{3,2,1,0:T(8,128)S(1)}, f32[2,1,64,128]{3,2,1,0:T(8,128)S(1)}, u32[]{:S(2)}, u32[]{:S(2)}) collective-permute-start(f32[2,1,64,128]{3,2,1,0:T(8,128)S(1)} %get-tuple-element.122), channel_id=1, source_target_pairs={{1,0},{2,1},{3,2},{5,4},{6,5},{7,6},{9,8},{10,9},{11,10},{13,12},{... | collective-permute-start | bytes 196616 | tf_op jit(solution)/shard_map/ppermute | solution.py:23
  99.4 0.8 copy-start.15
  103.7 5.6 %collective-permute-start.15 = (f32[2,1,64,128]{3,2,1,0:T(8,128)S(1)}, f32[2,1,64,128]{3,2,1,0:T(8,128)S(1)}, u32[]{:S(2)}, u32[]{:S(2)}) collective-permute-start(f32[2,1,64,128]{3,2,1,0:T(8,128)S(1)} %get-tuple-element.119), channel_id=1, source_target_pairs={{0,1},{1,2},{2,3},{4,5},{5,6},{6,7},{8,9},{9,10},{10,11},{12,13},{... | collective-permute-start | bytes 196616 | tf_op jit(solution)/shard_map/ppermute | solution.py:20
  108.1 3.1 %collective-permute-start.14 = (f32[2,1,64,128]{3,2,1,0:T(8,128)S(1)}, f32[2,1,64,128]{3,2,1,0:T(8,128)S(1)}, u32[]{:S(2)}, u32[]{:S(2)}) collective-permute-start(f32[2,1,64,128]{3,2,1,0:T(8,128)S(1)} %get-tuple-element.120), channel_id=1, source_target_pairs={{1,0},{2,1},{3,2},{5,4},{6,5},{7,6},{9,8},{10,9},{11,10},{13,12},{... | collective-permute-start | bytes 196616 | tf_op jit(solution)/shard_map/ppermute | solution.py:23
  111.2 1.0 copy-start.16
  111.7 1.1 copy-start.4
  111.7 1.2 copy-start.6
  111.7 1.4 copy-start.8
  111.7 1.5 copy-start.10
  111.7 1.7 %copy-start.12 = (f32[2,8,64,128]{3,2,1,0:T(8,128)S(1)}, f32[2,8,64,128]{3,2,1,0:T(8,128)}, u32[]{:S(2)}) copy-start(f32[2,8,64,128]{3,2,1,0:T(8,128)} %copy-done.11) | copy-start | bytes 1572868
  111.7 1.8 %copy-start.14 = (f32[2,8,64,128]{3,2,1,0:T(8,128)S(1)}, f32[2,8,64,128]{3,2,1,0:T(8,128)}, u32[]{:S(2)}) copy-start(f32[2,8,64,128]{3,2,1,0:T(8,128)} %copy-done.13) | copy-start | bytes 1572868
  113.5 1.2 copy-start.2
  119.0 28.2 %collective-permute-start.17 = (f32[1,1,64,128]{3,2,1,0:T(8,128)S(1)}, f32[1,1,64,128]{3,2,1,0:T(8,128)S(1)}, u32[]{:S(2)}, u32[]{:S(2)}) collective-permute-start(f32[1,1,64,128]{3,2,1,0:T(8,128)S(1)} %get-tuple-element.135), channel_id=1, source_target_pairs={{0,1},{1,2},{2,3},{4,5},{5,6},{6,7},{8,9},{9,10},{10,11},{12,13},{... | collective-permute-start | bytes 98312 | tf_op jit(solution)/shard_map/ppermute | solution.py:20
  123.4 23.8 %collective-permute-start.16 = (f32[1,1,64,128]{3,2,1,0:T(8,128)S(1)}, f32[1,1,64,128]{3,2,1,0:T(8,128)S(1)}, u32[]{:S(2)}, u32[]{:S(2)}) collective-permute-start(f32[1,1,64,128]{3,2,1,0:T(8,128)S(1)} %get-tuple-element.136), channel_id=1, source_target_pairs={{1,0},{2,1},{3,2},{5,4},{6,5},{7,6},{9,8},{10,9},{11,10},{13,12},{... | collective-permute-start | bytes 98312 | tf_op jit(solution)/shard_map/ppermute | solution.py:23
  126.1 29.9 %copy-start.18 = (f32[65536]{0:T(1024)}, f32[65536]{0:T(1024)S(1)}, u32[]{:S(2)}) copy-start(f32[65536]{0:T(1024)S(1)} %scatter_fusion.7) | copy-start | bytes 786436
Sparse Core Ops, SparseCore 0:
  114.9 30.3 all-gather.1
